TPU v7x, 128 devices: a whole 4x4x4 slice. The times are simulated.
128 devices in a mesh: fx: 16 (over x, z), fy: 8 (over y, core).
Axes of the slice: x: 4, y: 4, z: 4, core: 2. Of those that a mesh axis runs over, the one named last changes fastest.
Arguments:
- fluid_state: float32 [5, 8, 2048, 1024], P(None, None, 'fx', 'fy'), may hold values from -0.3 to 2.8, as said below
- surface_points: float32 [16384, 3, 128], P(('fx', 'fy')), may hold values from 0 to 1
- surface_normals: float32 [16384, 3, 128], P(('fx', 'fy')), may hold values from -1 to 1
- owner_ids: int32 [16384, 1], P(('fx', 'fy')), may hold values from 0 to 127; in each aligned block of 128 rows (0 to 127, 128 to 255, ...) at most 2 rows name the same one
- support_ids: int32 [16384, 2], P(('fx', 'fy')), may hold values from 0 to 7
- struct_points: float32 [1024, 3, 128], P(('fx', 'fy')), may hold values from 0 to 1
- couplings: float32 [1024, 4, 128, 128], P(('fx', 'fy')), may hold values from 0.5 to 1
- coupling_pattern: int32 [1024, 4], P(('fx', 'fy')), may hold values from 0 to 7, as said below
- stiff_diagonal: float32 [1024, 128], P(('fx', 'fy')), may hold values from 1.05 to 1.6
- struct_load: float32 [1024, 3, 128], P(('fx', 'fy')), may hold values from -6 to 6
- predicted: float32 [1024, 3, 128], P(('fx', 'fy')), may hold values from -3 to 3
- hist_residual: float32 [8, 1024, 3, 128], P(None, ('fx', 'fy')), may hold values from -0.03 to 0.03
- hist_response: float32 [8, 1024, 3, 128], P(None, ('fx', 'fy')), may hold values from -6 to 6
Outputs:
- new_state: float32 [5, 8, 2048, 1024], P(None, None, 'fx', 'fy')
- next_estimate: float32 [1024, 3, 128], P(('fx', 'fy'))
- coupling_residual: float32 [1024, 3, 128], P(('fx', 'fy'))
Inputs may be any that keep to these rules, and one draw needn't show every extreme that they name: `fluid_state`: component 0 (density) lies in [0.8, 1.2], components 1 to 3 (momenta) in [-0.3, 0.3], component 4 (total energy) in [2.2, 2.8]. `owner_ids`: among the 128 surface blocks of one device (aligned blocks of rows), no owner is named by more than 2 of them. `support_ids`: local block numbers on the owner. For each device's 8 structure blocks and each column k, the entries coupling_pattern[., k] are a permutation of 0 to 7.
All inputs are finite; a program needn't handle non-finite values.
Results may differ from a plain program's by a relative error of at most 0.0003.
Values sent between devices are 32-bit elements; how exact they have to be, the bound alone decides.
No kernel may reach another device: no remote copies, remote signals or barrier semaphores. Data moves between devices by JAX's collectives and lax.ppermute only.
A program may use at most 192 MiB of HBM per device.

v0:
```python
import math
import jax
import jax.numpy as jnp
from jax import lax
from jax.sharding import PartitionSpec as P

CG_ITERS = 2
COUPLE = 2
TOP_PRECISION = lax.Precision.HIGHEST
STEP_RATIO = 0.12
WALL_SPEED = 0.5
WALL_GAIN = 0.5
LOAD_SCALE = 4.0
PRESSURE_REF = 0.98
RADIUS = 1.0


def with_halo(cells, sides, width):
    for axis, dim in sides:
        count = lax.axis_size(axis)
        head = lax.slice_in_dim(cells, 0, width, axis=dim)
        tail = lax.slice_in_dim(cells, cells.shape[dim] - width, cells.shape[dim], axis=dim)
        cells = jnp.concatenate(
            [
                lax.ppermute(tail, axis, [(i, (i + 1) % count) for i in range(count)]),
                cells,
                lax.ppermute(head, axis, [((i + 1) % count, i) for i in range(count)]),
            ],
            axis=dim,
        )
    return cells


def state_pressure(state):
    return 0.4 * (
        state[4]
        - 0.5 * (state[1] * state[1] + state[2] * state[2] + state[3] * state[3]) / state[0]
    )


def face_terms(state, momentum):
    density = state[0]
    velocity = state[momentum] / density
    pressure = state_pressure(state)
    flux = state * velocity
    flux = flux.at[momentum].add(pressure)
    flux = flux.at[4].add(pressure * velocity)
    speed = jnp.abs(velocity) + jnp.sqrt(1.4 * pressure / density)
    return (flux, speed)


def rusanov(left, right, left_flux, right_flux, left_speed, right_speed):
    return 0.5 * (left_flux + right_flux) - 0.5 * jnp.maximum(left_speed, right_speed) * (
        right - left
    )


def vertical_terms(state, wall):
    bottom = state[:, 0]
    ghost = bottom.at[3].set(2.0 * bottom[0] * wall - bottom[3])
    column = jnp.concatenate([ghost[:, None], state, state[:, -1:]], axis=1)
    flux, speed = face_terms(column, 3)
    faces = rusanov(column[:, :-1], column[:, 1:], flux[:, :-1], flux[:, 1:], speed[:-1], speed[1:])
    return faces[:, 1:] - faces[:, :-1]


def horizontal_terms(state):
    extended = with_halo(state, (("fx", 2), ("fy", 3)), 1)
    strip = extended[:, :, :, 1:-1]
    flux, speed = face_terms(strip, 1)
    faces = rusanov(
        strip[:, :, :-1],
        strip[:, :, 1:],
        flux[:, :, :-1],
        flux[:, :, 1:],
        speed[:, :-1],
        speed[:, 1:],
    )
    total = faces[:, :, 1:] - faces[:, :, :-1]
    strip = extended[:, :, 1:-1, :]
    flux, speed = face_terms(strip, 2)
    faces = rusanov(
        strip[:, :, :, :-1],
        strip[:, :, :, 1:],
        flux[:, :, :, :-1],
        flux[:, :, :, 1:],
        speed[:, :, :-1],
        speed[:, :, 1:],
    )
    return total + (faces[:, :, :, 1:] - faces[:, :, :, :-1])


def kernel_block(fluid_points, struct_nodes):
    squared = jnp.zeros((), jnp.float32)
    for axis in range(3):
        offset = fluid_points[..., axis, :, None] - struct_nodes[..., axis, None, :]
        squared = squared + offset * offset
    ratio = jnp.sqrt(squared) / RADIUS
    reach = jnp.maximum(1.0 - ratio, 0.0)
    return reach * reach * reach * reach * (4.0 * ratio + 1.0)


def owner_kernels(places, support, struct_points):
    rows = places.shape[0]
    points = places.shape[-1]
    spread = support.shape[1]
    group = math.gcd(rows, 16)

    def one_group(inputs):
        where, which = inputs
        return kernel_block(where[:, None], struct_points[which])

    kernels = lax.map(
        one_group, (places.reshape(-1, group, 3, points), support.reshape(-1, group, spread))
    )
    return kernels.reshape(rows, spread, points, points)


def owner_motion(kernels, support, field_values):
    return jnp.einsum("gkij,gkcj->gci", kernels, field_values[support], precision=TOP_PRECISION)


def owner_loads(kernels, support, blocks, traction):
    flux_terms = jnp.einsum("gkij,gci->gkcj", kernels, traction, precision=TOP_PRECISION)
    selector = (support[:, :, None] == jnp.arange(blocks, dtype=jnp.int32)[None, None, :]).astype(
        jnp.float32
    )
    return jnp.einsum("rke,rkcj->ecj", selector, flux_terms, precision=TOP_PRECISION)


def route_coords(geometry, support):
    moved_geometry, moved_support = (
        lax.all_to_all(geometry, ("fx", "fy"), split_axis=0, concat_axis=0, tiled=True),
        lax.all_to_all(support, ("fx", "fy"), split_axis=0, concat_axis=0, tiled=True),
    )
    return (moved_geometry, moved_support)


def route_field(values):
    return lax.all_to_all(values, ("fx", "fy"), split_axis=0, concat_axis=0, tiled=True)


def global_sums(values):
    return lax.psum(values, ("fx", "fy"))


def stiffness(field_values, couplings, sparsity_layout, selector, diagonal):
    blocks = field_values.shape[0]
    scale = 1.0 / (2.0 * couplings.shape[1] * couplings.shape[2])
    flux_terms = jnp.einsum("aosq,avs->aovq", couplings, field_values, precision=TOP_PRECISION)
    shipped = jnp.einsum("bke,bkdj->edj", selector, flux_terms, precision=TOP_PRECISION)
    stacked = jnp.concatenate([shipped, field_values], axis=0)
    extended = with_halo(stacked, ((("fx", "fy"), 0),), blocks)
    prior_iterate = extended[:blocks]
    later = extended[-blocks:]
    forward_pass = jnp.einsum(
        "hzwm,hzlm->hlw", couplings, prior_iterate[sparsity_layout], precision=TOP_PRECISION
    )
    return diagonal[:, None, :] * field_values - scale * (forward_pass + later)


def conjugate(start, rhs, operate):
    residual = rhs - operate(start)
    solution = start
    direction = residual
    norm_now = global_sums(jnp.stack([jnp.sum(residual * residual)]))[0]
    for count in range(CG_ITERS):
        image = operate(direction)
        alpha = norm_now / global_sums(jnp.stack([jnp.sum(direction * image)]))[0]
        solution = solution + alpha * direction
        residual = residual - alpha * image
        if count + 1 < CG_ITERS:
            norm_next = global_sums(jnp.stack([jnp.sum(residual * residual)]))[0]
            direction = residual + norm_next / norm_now * direction
            norm_now = norm_next
    return solution


def newton_update(response, gram, projected, responses):
    lower = jnp.linalg.cholesky(gram)
    middle = lax.linalg.triangular_solve(lower, projected[:, None], left_side=True, lower=True)
    weights = lax.linalg.triangular_solve(
        lower, middle, left_side=True, lower=True, transpose_a=True
    )[:, 0]
    return response - jnp.einsum("h,hbdp->bdp", weights, responses, precision=TOP_PRECISION)


def on_device(
    fluid_state,
    surface_points,
    surface_normals,
    owner_ids,
    support_ids,
    struct_points,
    couplings,
    coupling_pattern,
    stiff_diagonal,
    struct_load,
    predicted,
    hist_residual,
    hist_response,
):
    rows_fx = lax.axis_size("fx")
    rows_fy = lax.axis_size("fy")
    devices = rows_fx * rows_fy
    surface_count = owner_ids.shape[0]
    capacity = max(2, 2 * surface_count // devices)
    owners = owner_ids[:, 0]
    chosen = (owners[:, None] == jnp.arange(devices, dtype=jnp.int32)[None, :]).astype(jnp.int32)
    slots = owners * capacity + jnp.sum((jnp.cumsum(chosen, axis=0) - chosen) * chosen, axis=1)
    width = devices * capacity

    def pack(values):
        return jnp.zeros((width,) + values.shape[1:], values.dtype).at[slots].set(values)

    owner_geometry, owner_support = route_coords(pack(surface_points), pack(support_ids))
    kernels = owner_kernels(owner_geometry, owner_support, struct_points)
    blocks = couplings.shape[0]
    selector = (
        coupling_pattern[:, :, None] == jnp.arange(blocks, dtype=jnp.int32)[None, None, :]
    ).astype(jnp.float32)

    def operate(field_values):
        return stiffness(field_values, couplings, coupling_pattern, selector, stiff_diagonal)

    horizontal = horizontal_terms(fluid_state)
    estimate = predicted
    differences = hist_residual
    responses = hist_response
    last_residual = predicted
    last_response = predicted
    new_state = fluid_state
    residual = predicted
    for count in range(COUPLE):
        motion_slots = owner_motion(kernels, owner_support, estimate)
        motion = route_field(motion_slots)[slots]
        wall = WALL_SPEED * jnp.tanh(WALL_GAIN * jnp.sum(surface_normals * motion, axis=1))
        new_state = fluid_state - STEP_RATIO * (horizontal + vertical_terms(fluid_state, wall))
        pressure = state_pressure(new_state[:, 0])
        traction = -LOAD_SCALE * (pressure - PRESSURE_REF)[:, None, :] * surface_normals
        owner_traction = route_field(pack(traction))
        loads = owner_loads(kernels, owner_support, blocks, owner_traction)
        response = conjugate(estimate, struct_load + loads, operate)
        residual = response - estimate
        if count > 0:
            differences = jnp.concatenate(
                [differences[1:], (residual - last_residual)[None]], axis=0
            )
            responses = jnp.concatenate([responses[1:], (response - last_response)[None]], axis=0)
        last_residual = residual
        last_response = response
        gram = jnp.einsum("hbdp,gbdp->hg", differences, differences, precision=TOP_PRECISION)
        projected = jnp.einsum("hbdp,bdp->h", differences, residual, precision=TOP_PRECISION)
        totals = global_sums(jnp.concatenate([gram, projected[:, None]], axis=1))
        estimate = newton_update(response, totals[:, :-1], totals[:, -1], responses)
    return (new_state, estimate, residual)


def solution(mesh):
    placed = (
        P(None, None, "fx", "fy"),
        P(("fx", "fy"), None, None),
        P(("fx", "fy"), None, None),
        P(("fx", "fy"), None),
        P(("fx", "fy"), None),
        P(("fx", "fy"), None, None),
        P(("fx", "fy"), None, None, None),
        P(("fx", "fy"), None),
        P(("fx", "fy"), None),
        P(("fx", "fy"), None, None),
        P(("fx", "fy"), None, None),
        P(None, ("fx", "fy"), None, None),
        P(None, ("fx", "fy"), None, None),
    )
    return jax.shard_map(
        on_device,
        mesh=mesh,
        in_specs=placed,
        out_specs=(
            P(None, None, "fx", "fy"),
            P(("fx", "fy"), None, None),
            P(("fx", "fy"), None, None),
        ),
        check_vma=False,
    )
```

profile of v0, /device:TPU:1, one launch (start us, length us, event | category | flops | bytes accessed | tf_op | source)
XLA Modules:
  0.0 1005.2 jit_solution(8151141601063758827)
XLA Ops:
  6.5 11.5 %all-to-all-start = ((s32[128,2,2]{1,2,0:T(2,128)}), s32[128,2,2]{1,2,0:T(2,128)S(1)}, u32[]{:S(2)}, u32[]{:S(2)}) async-start(s32[128,2,2]{1,2,0:T(2,128)} %copy.261), calls=%async_computation | async-start | bytes 262144 | tf_op jit(solution)/shard_map/all_to_all | solution.py:134
  19.6 5.4 collective-permute-start.1
  32.7 12.5 %scatter_fusion = f32[256,3,128]{2,1,0:T(4,128)} fusion(f32[256,3,128]{2,1,0:T(4,128)} %broadcast.438.clone, s32[128]{0:T(128)S(1)} %fusion.166, f32[128,3,128]{2,1,0:T(4,128)S(1)} %copy.265), kind=kCustom, calls=%fused_computation.12 | custom fusion | bytes 590336 | tf_op jit(solution)/shard_map/scatter | solution.py:214
  45.2 15.0 %all-to-all-start.1 = ((f32[256,3,128]{2,1,0:T(4,128)}), f32[256,3,128]{2,1,0:T(4,128)}, u32[]{:S(2)}, u32[]{:S(2)}) async-start(f32[256,3,128]{2,1,0:T(4,128)} %scatter_fusion), calls=%async_computation.1 | async-start | bytes 1048576 | tf_op jit(solution)/shard_map/all_to_all | solution.py:133
  65.0 3.3 fusion.182
  70.4 3.3 copy.253
  75.3 3.9 copy.254
  87.1 3.2 copy.255
  93.6 5.9 pad_maximum_fusion
  112.6 69.3 %while.20 = (s32[]{:T(128)}, f32[16,16,2,128,128]{4,3,2,1,0:T(8,128)}, f32[16,16,3,128]{3,1,2,0:T(8,128)}, s32[16,16,2]{1,0,2:T(8,128)S(1)}, f32[8,3,128]{2,1,0:T(4,128)S(1)}, /*index=5*/s32[]{:T(128)}) while((s32[]{:T(128)}, f32[16,16,2,128,128]{4,3,2,1,0:T(8,128)}, f32[16,16,3,128]{3,1,2,0:T(8,128)}, s32[16,16,2]{1,0,2:T(8,128)S(1)}, ...), condition=%wide.region_5.6_spmd, body=%wide.region_4.5_spmd.sunk | while | flops 8389730 | bytes 2471257 | solution.py:113
  182.0 32.0 %convolution_bitcast_fusion.3 = f32[256,3,128]{2,1,0:T(4,128)} fusion(f32[256,2,128,128]{3,2,1,0:T(8,128)} %bitcast.465, f32[256,2,3,128]{3,1,0,2:T(2,128)S(1)} %bitcast.471), kind=kOutput, calls=%fused_computation.76 | convolution fusion | flops 301989888 | bytes 34734080 | tf_op jit(solution)/shard_map/gkij,gkcj->gci/dot_general | solution.py:120
  213.9 10.2 %all-to-all-start.2 = ((f32[256,3,128]{2,1,0:T(4,128)}), f32[256,3,128]{2,1,0:T(4,128)}, u32[]{:S(2)}, u32[]{:S(2)}) async-start(f32[256,3,128]{2,1,0:T(4,128)} %convolution_bitcast_fusion.3), calls=%async_computation.2 | async-start | bytes 1048576 | tf_op jit(solution)/shard_map/all_to_all | solution.py:140
  224.2 11.7 %fusion.4 = f32[5,8,128,129]{3,2,1,0:T(8,128)} fusion(f32[5,8,130,1]{3,2,1,0:T(8,128)} %copy.255, f32[5,8,1,128]{3,2,1,0:T(1,128)S(1)} %bitcast.482, f32[5,8,128,128]{3,2,1,0:T(8,128)} %param.40, f32[5,8,1,128]{3,2,1,0:T(1,128)S(1)} %bitcast.487, f32[5,8,130,1]{3,2,1,0:T(8,128)} %copy.256, f32[5,8,128,130]{3,2,1,0:T(8,128)} %fusion.25, f32[8,128,129]{2,1,0:T(8,128)} %fusion.24), kind=kLoop, calls=%fused_computation.29 | loop fusion | flops 7265280 | bytes 11158144 | tf_op jit(solution)/shard_map/sub | solution.py:53
  252.1 12.4 %scatter_fusion.1 = f32[256,3,128]{2,1,0:T(4,128)} fusion(f32[256,3,128]{2,1,0:T(4,128)} %broadcast.438.clone.1, s32[128]{0:T(128)S(1)} %fusion.166, f32[128,3,128]{2,1,0:T(4,128)S(1)} %copy.273), kind=kCustom, calls=%fused_computation.13 | custom fusion | bytes 590336 | tf_op jit(solution)/shard_map/scatter | solution.py:214
  264.5 9.2 all-to-all-start.3
  276.7 10.5 %all-to-all-done.3 = f32[256,3,128]{2,1,0:T(4,128)S(1)} async-done(((f32[256,3,128]{2,1,0:T(4,128)}), f32[256,3,128]{2,1,0:T(4,128)S(1)}, u32[]{:S(2)}, u32[]{:S(2)}) %all-to-all-start.3) | async-done | bytes 393248 | tf_op jit(solution)/shard_map/all_to_all | solution.py:140
  287.2 19.6 %convolution_bitcast_fusion.1 = f32[256,2,3,128]{3,2,1,0:T(4,128)S(1)} fusion(f32[256,2,128,128]{3,2,1,0:T(8,128)} %bitcast.466, f32[256,3,128]{2,1,0:T(4,128)S(1)} %all-to-all-done.3), kind=kOutput, calls=%fused_computation.74 | convolution fusion | flops 301989888 | bytes 34734080 | tf_op jit(solution)/shard_map/gkij,gci->gkcj/dot_general | solution.py:124
  314.2 71.7 %all-reduce.1 = (f32[1]{0:T(128)}, f32[1]{0:T(128)}) all-reduce(f32[1]{0:T(128)} %bitcast.55, f32[1]{0:T(128)} %bitcast.63), channel_id=1, replica_groups=mesh['fx'=16,'fy'=8] {'fx','fy'}, use_global_device_ids=true, to_apply=%region_9.10 | all-reduce | flops 2 | bytes 16 | tf_op jit(solution)/shard_map/psum | solution.py:144
  388.0 62.7 %psum.72 = f32[1]{0:T(128)} all-reduce(f32[1]{0:T(128)} %bitcast.65), channel_id=1, replica_groups=mesh['fx'=16,'fy'=8] {'fx','fy'}, use_global_device_ids=true, to_apply=%region_13.14 | all-reduce | flops 1 | bytes 8 | tf_op jit(solution)/shard_map/psum | solution.py:144
  459.2 70.4 %psum.73 = f32[1]{0:T(128)} all-reduce(f32[1]{0:T(128)} %bitcast.74), channel_id=1, replica_groups=mesh['fx'=16,'fy'=8] {'fx','fy'}, use_global_device_ids=true, to_apply=%region_15.16 | all-reduce | flops 1 | bytes 8 | tf_op jit(solution)/shard_map/psum | solution.py:144
  531.3 62.6 %psum.74 = f32[8,9]{0,1:T(8,128)S(1)} all-reduce(f32[8,9]{0,1:T(8,128)S(1)} %pad_maximum_fusion.17), channel_id=1, replica_groups=mesh['fx'=16,'fy'=8] {'fx','fy'}, use_global_device_ids=true, to_apply=%region_16.17 | all-reduce | flops 72 | bytes 576 | tf_op jit(solution)/shard_map/psum | solution.py:144
  599.2 31.6 %convolution_bitcast_fusion.2 = f32[256,3,128]{2,1,0:T(4,128)} fusion(f32[256,2,3,128]{3,2,1,0:T(4,128)S(1)} %bitcast.472, f32[256,2,128,128]{3,2,1,0:T(8,128)} %bitcast.467), kind=kOutput, calls=%fused_computation.75 | convolution fusion | flops 301989888 | bytes 34734080 | tf_op jit(solution)/shard_map/gkij,gkcj->gci/dot_general | solution.py:120
  630.9 5.4 all-to-all-start.4
  639.1 10.9 %all-to-all-done.4 = f32[256,3,128]{2,1,0:T(4,128)S(1)} async-done(((f32[256,3,128]{2,1,0:T(4,128)}), f32[256,3,128]{2,1,0:T(4,128)S(1)}, u32[]{:S(2)}, u32[]{:S(2)}) %all-to-all-start.4) | async-done | bytes 393248 | tf_op jit(solution)/shard_map/all_to_all | solution.py:140
  664.4 12.4 %scatter_fusion.2 = f32[256,3,128]{2,1,0:T(4,128)} fusion(f32[256,3,128]{2,1,0:T(4,128)} %broadcast.438, s32[128]{0:T(128)S(1)} %copy-done.27, f32[128,3,128]{2,1,0:T(4,128)S(1)} %copy.296), kind=kCustom, calls=%fused_computation.14 | custom fusion | bytes 590336 | tf_op jit(solution)/shard_map/scatter | solution.py:214
  676.8 4.6 all-to-all-start.5
  686.7 8.3 all-to-all-done.5
  695.0 19.6 %convolution_bitcast_fusion = f32[256,2,3,128]{3,2,1,0:T(4,128)S(1)} fusion(f32[256,2,128,128]{3,2,1,0:T(8,128)} %bitcast.468, f32[256,3,128]{2,1,0:T(4,128)S(1)} %all-to-all-done.5), kind=kOutput, calls=%fused_computation.73 | convolution fusion | flops 301989888 | bytes 34734080 | tf_op jit(solution)/shard_map/gkij,gci->gkcj/dot_general | solution.py:124
  721.3 71.7 %all-reduce = (f32[1]{0:T(128)}, f32[1]{0:T(128)}) all-reduce(f32[1]{0:T(128)} %bitcast.119, f32[1]{0:T(128)} %bitcast.127), channel_id=1, replica_groups=mesh['fx'=16,'fy'=8] {'fx','fy'}, use_global_device_ids=true, to_apply=%region_22.26 | all-reduce | flops 2 | bytes 16 | tf_op jit(solution)/shard_map/psum | solution.py:144
  795.0 62.5 %psum.77 = f32[1]{0:T(128)} all-reduce(f32[1]{0:T(128)} %bitcast.129), channel_id=1, replica_groups=mesh['fx'=16,'fy'=8] {'fx','fy'}, use_global_device_ids=true, to_apply=%region_26.30 | all-reduce | flops 1 | bytes 8 | tf_op jit(solution)/shard_map/psum | solution.py:144
  866.1 70.4 %psum.78 = f32[1]{0:T(128)} all-reduce(f32[1]{0:T(128)} %bitcast.138), channel_id=1, replica_groups=mesh['fx'=16,'fy'=8] {'fx','fy'}, use_global_device_ids=true, to_apply=%region_28.32 | all-reduce | flops 1 | bytes 8 | tf_op jit(solution)/shard_map/psum | solution.py:144
  938.5 62.6 %psum.79 = f32[8,9]{0,1:T(8,128)S(1)} all-reduce(f32[8,9]{0,1:T(8,128)S(1)} %pad_maximum_fusion.18), channel_id=1, replica_groups=mesh['fx'=16,'fy'=8] {'fx','fy'}, use_global_device_ids=true, to_apply=%region_29.33 | all-reduce | flops 72 | bytes 576 | tf_op jit(solution)/shard_map/psum | solution.py:144
  (414 shorter events, 197.7 us)
Async XLA Ops:
  0.7 30.9 %copy-start.18 = (f32[128,3,128]{2,0,1:T(8,128)S(1)}, f32[128,3,128]{2,0,1:T(8,128)}, u32[]{:S(2)}) copy-start(f32[128,3,128]{2,0,1:T(8,128)} %param.41) | copy-start | bytes 589828
  3.3 248.8 %copy-start.26 = (s32[128]{0:T(128)}, s32[128]{0:T(128)S(1)}, u32[]{:S(2)}) copy-start(s32[128]{0:T(128)S(1)} %fusion.166) | copy-start | bytes 1540
  6.5 38.7 %all-to-all-start = ((s32[128,2,2]{1,2,0:T(2,128)}), s32[128,2,2]{1,2,0:T(2,128)S(1)}, u32[]{:S(2)}, u32[]{:S(2)}) async-start(s32[128,2,2]{1,2,0:T(2,128)} %copy.261), calls=%async_computation | async-start | bytes 262144 | tf_op jit(solution)/shard_map/all_to_all | solution.py:134
  19.6 43.4 %collective-permute-start.1 = (f32[5,8,1,128]{3,1,2,0:T(8,128)}, f32[5,8,1,128]{3,1,2,0:T(8,128)S(1)}, u32[]{:S(2)}, u32[]{:S(2)}) collective-permute-start(f32[5,8,1,128]{3,1,2,0:T(8,128)} %bitcast.176), channel_id=1, source_target_pairs={{8,0},{16,8},{24,16},{32,24},{40,32},{48,40},{56,48},{64,56},{72,6... | collective-permute-start | bytes 61448 | tf_op jit(solution)/shard_map/ppermute | solution.py:27
  25.0 38.0 %collective-permute-start = (f32[5,8,1,128]{3,1,2,0:T(8,128)}, f32[5,8,1,128]{3,1,2,0:T(8,128)S(1)}, u32[]{:S(2)}, u32[]{:S(2)}) collective-permute-start(f32[5,8,1,128]{3,1,2,0:T(8,128)} %bitcast.175), channel_id=1, source_target_pairs={{0,8},{8,16},{16,24},{24,32},{32,40},{40,48},{48,56},{56,64},{64,7... | collective-permute-start | bytes 61448 | tf_op jit(solution)/shard_map/ppermute | solution.py:25
  27.7 279.1 %collective-permute-start.5 = (f32[8,3,128]{2,0,1:T(8,128)}, f32[8,3,128]{2,0,1:T(8,128)}, u32[]{:S(2)}, u32[]{:S(2)}) collective-permute-start(f32[8,3,128]{2,0,1:T(8,128)} %convolution_bitcast_fusion.22), channel_id=1, source_target_pairs={{1,0},{2,1},{3,2},{4,3},{5,4},{6,5},{7,6},{8,7},{9,8},{10,9},{11,1... | collective-permute-start | bytes 36872 | tf_op jit(solution)/shard_map/ppermute | solution.py:27
  28.3 245.9 %collective-permute-start.4 = (f32[8,3,128]{2,1,0:T(4,128)S(1)}, f32[8,3,128]{2,1,0:T(4,128)S(1)}, u32[]{:S(2)}, u32[]{:S(2)}) collective-permute-start(f32[8,3,128]{2,1,0:T(4,128)S(1)} %copy.275), channel_id=1, source_target_pairs={{0,1},{1,2},{2,3},{3,4},{4,5},{5,6},{6,7},{7,8},{8,9},{9,10},{10,1... | collective-permute-start | bytes 36872 | tf_op jit(solution)/shard_map/ppermute | solution.py:25
  30.7 30.1 %copy-start.9 = (f32[5,1,128,128]{3,2,1,0:T(8,128)}, f32[5,1,128,128]{3,2,1,0:T(8,128)S(1)}, u32[]{:S(2)}) copy-start(f32[5,1,128,128]{3,2,1,0:T(8,128)S(1)} %get-tuple-element.226) | copy-start | bytes 983044
  30.7 206.5 %copy-start.28 = (s32[1024]{0:T(1024)}, s32[1024]{0:T(1024)S(1)}, u32[]{:S(2)}) copy-start(s32[1024]{0:T(1024)S(1)} %pad_clamp_fusion.2) | copy-start | bytes 12292
  45.2 65.6 %all-to-all-start.1 = ((f32[256,3,128]{2,1,0:T(4,128)}), f32[256,3,128]{2,1,0:T(4,128)}, u32[]{:S(2)}, u32[]{:S(2)}) async-start(f32[256,3,128]{2,1,0:T(4,128)} %scatter_fusion), calls=%async_computation.1 | async-start | bytes 1048576 | tf_op jit(solution)/shard_map/all_to_all | solution.py:133
  73.7 13.5 %collective-permute-start.2 = (f32[5,8,130,1]{2,1,3,0:T(8,128)S(1)}, f32[5,8,130,1]{2,1,3,0:T(8,128)}, u32[]{:S(2)}, u32[]{:S(2)}) collective-permute-start(f32[5,8,130,1]{2,1,3,0:T(8,128)S(1)} %copy.253), channel_id=1, source_target_pairs={{0,1},{1,2},{2,3},{3,4},{4,5},{5,6},{6,7},{7,0},{8,9},{9,10},{10,1... | collective-permute-start | bytes 62408 | tf_op jit(solution)/shard_map/ppermute | solution.py:25
  79.2 11.2 %collective-permute-start.3 = (f32[5,8,130,1]{2,1,3,0:T(8,128)}, f32[5,8,130,1]{2,1,3,0:T(8,128)}, u32[]{:S(2)}, u32[]{:S(2)}) collective-permute-start(f32[5,8,130,1]{2,1,3,0:T(8,128)} %copy.254), channel_id=1, source_target_pairs={{1,0},{2,1},{3,2},{4,3},{5,4},{6,5},{7,6},{0,7},{9,8},{10,9},{11,1... | collective-permute-start | bytes 62408 | tf_op jit(solution)/shard_map/ppermute | solution.py:27
  213.9 23.2 %all-to-all-start.2 = ((f32[256,3,128]{2,1,0:T(4,128)}), f32[256,3,128]{2,1,0:T(4,128)}, u32[]{:S(2)}, u32[]{:S(2)}) async-start(f32[256,3,128]{2,1,0:T(4,128)} %convolution_bitcast_fusion.3), calls=%async_computation.2 | async-start | bytes 1048576 | tf_op jit(solution)/shard_map/all_to_all | solution.py:140
  264.5 22.7 %all-to-all-start.3 = ((f32[256,3,128]{2,1,0:T(4,128)}), f32[256,3,128]{2,1,0:T(4,128)S(1)}, u32[]{:S(2)}, u32[]{:S(2)}) async-start(f32[256,3,128]{2,1,0:T(4,128)} %scatter_fusion.1), calls=%async_computation.3 | async-start | bytes 1048576 | tf_op jit(solution)/shard_map/all_to_all | solution.py:140
  274.3 32.6 %copy-start.23 = (s32[256,2]{0,1:T(2,128)}, s32[256,2]{0,1:T(2,128)S(1)}, u32[]{:S(2)}) copy-start(s32[256,2]{0,1:T(2,128)S(1)} %eq.26) | copy-start | bytes 6148
  276.7 30.1 %copy-start.19 = (f32[8,128]{1,0:T(8,128)S(1)}, f32[8,128]{1,0:T(8,128)}, u32[]{:S(2)}) copy-start(f32[8,128]{1,0:T(8,128)} %param.48) | copy-start | bytes 12292
  276.7 30.1 %copy-start.22 = (f32[8,3,128]{2,0,1:T(8,128)S(1)}, f32[8,3,128]{2,0,1:T(8,128)}, u32[]{:S(2)}) copy-start(f32[8,3,128]{2,0,1:T(8,128)} %param.49) | copy-start | bytes 36868
  308.0 2.5 collective-permute-start.6
  310.5 3.1 collective-permute-start.7
  312.9 283.9 %copy-start.17 = (f32[8,8,3,128]{3,1,2,0:T(8,128)S(1)}, f32[8,8,3,128]{3,1,2,0:T(8,128)}, u32[]{:S(2)}) copy-start(f32[8,8,3,128]{3,1,2,0:T(8,128)} %param.52) | copy-start | bytes 294916
  452.1 3.0 collective-permute-start.8
  455.1 3.4 collective-permute-start.9
  630.9 19.1 %all-to-all-start.4 = ((f32[256,3,128]{2,1,0:T(4,128)}), f32[256,3,128]{2,1,0:T(4,128)S(1)}, u32[]{:S(2)}, u32[]{:S(2)}) async-start(f32[256,3,128]{2,1,0:T(4,128)} %convolution_bitcast_fusion.2), calls=%async_computation.4 | async-start | bytes 1048576 | tf_op jit(solution)/shard_map/all_to_all | solution.py:140
  637.1 47.1 %collective-permute-start.10 = (f32[8,3,128]{2,0,1:T(8,128)S(1)}, f32[8,3,128]{2,0,1:T(8,128)S(1)}, u32[]{:S(2)}, u32[]{:S(2)}) collective-permute-start(f32[8,3,128]{2,0,1:T(8,128)S(1)} %bitcast_subtract_fusion.1), channel_id=1, source_target_pairs={{0,1},{1,2},{2,3},{3,4},{4,5},{5,6},{6,7},{7,8},{8,9},{9,10},{10,1... | collective-permute-start | bytes 36872 | tf_op jit(solution)/shard_map/ppermute | solution.py:25
  676.8 18.1 %all-to-all-start.5 = ((f32[256,3,128]{2,1,0:T(4,128)}), f32[256,3,128]{2,1,0:T(4,128)S(1)}, u32[]{:S(2)}, u32[]{:S(2)}) async-start(f32[256,3,128]{2,1,0:T(4,128)} %scatter_fusion.2), calls=%async_computation.5 | async-start | bytes 1048576 | tf_op jit(solution)/shard_map/all_to_all | solution.py:140
  682.8 31.9 %collective-permute-start.11 = (f32[8,3,128]{2,0,1:T(8,128)S(1)}, f32[8,3,128]{2,0,1:T(8,128)S(1)}, u32[]{:S(2)}, u32[]{:S(2)}) collective-permute-start(f32[8,3,128]{2,0,1:T(8,128)S(1)} %convolution_bitcast_fusion.18), channel_id=1, source_target_pairs={{1,0},{2,1},{3,2},{4,3},{5,4},{6,5},{7,6},{8,7},{9,8},{10,9},{11,1... | collective-permute-start | bytes 36872 | tf_op jit(solution)/shard_map/ppermute | solution.py:27
  715.1 2.5 collective-permute-start.12
  717.5 3.1 collective-permute-start.13
  720.0 284.1 %slice-start.2 = ((f32[8,8,3,128]{3,1,2,0:T(8,128)}), f32[7,8,3,128]{3,1,2,0:T(8,128)S(1)}, s32[]{:S(2)}) async-start(f32[8,8,3,128]{3,1,2,0:T(8,128)} %param.52), calls=%async_computation.8 | async-start | bytes 172032 | tf_op jit(solution)/shard_map/slice | solution.py:249
  858.9 3.2 collective-permute-start.14
  862.0 3.4 collective-permute-start.15
  937.8 67.2 %copy-start.21 = (f32[8,3,128]{2,0,1:T(8,128)}, f32[8,3,128]{2,0,1:T(8,128)S(1)}, u32[]{:S(2)}) copy-start(f32[8,3,128]{2,0,1:T(8,128)S(1)} %get-tuple-element.201) | copy-start | bytes 36868
  (22 other events, 221.2 us)
where the time goes:
time: 1010 us
  blocking collectives  535 us (53%)
  matrix products  127 us (13%)
  local copies, waits for them, and re-layouts  113 us (11%)
  other arithmetic  113 us (11%)
  starting transfers between devices  74.2 us (7%)
  waiting for transfers between devices  34.2 us (3%)
    psum x8, blocking collectives, global_sums(): return lax.psum(values, ('fx', 'fy'))  535 us
    dot_general x2, matrix products, owner_motion(): jnp.einsum('gkij,gkcj->gci', kernels, field_values[support], precision=TO...  63.6 us
    dynamic_update_slice x16, other arithmetic, owner_kernels(): lax.map(one_group, (places.reshape(-1, group, 3, points), support.reshape...  43.5 us
    dot_general x2, matrix products, owner_loads(): jnp.einsum('gkij,gci->gkcj', kernels, traction, precision=TOP_PRECISION)  39.3 us
    scatter x4, local copies, waits for them, and re-layouts, pack(): jnp.zeros((width,) + values.shape[1:], values.dtype).at[slots].set(values)  38.3 us
    all_to_all x4, waiting for transfers between devices, route_field(): lax.all_to_all(values, ('fx', 'fy'), split_axis=0, concat_axis=0, tiled=T...  30.9 us
    all_to_all x4, starting transfers between devices, route_field(): lax.all_to_all(values, ('fx', 'fy'), split_axis=0, concat_axis=0, tiled=T...  29.5 us
  transfers between devices with their start and end apart: 22, of which 8 were waited for; matrix products, arithmetic and copies ran while one was open for 29% of the time, Pallas kernels for 0%

commit v1 on v0

--- a/solution.py
+++ b/solution.py
@@ -1,3 +1,4 @@
+import functools
 import math
 import jax
 import jax.numpy as jnp
@@ -13,6 +14,13 @@
 LOAD_SCALE = 4.0
 PRESSURE_REF = 0.98
 RADIUS = 1.0
+
+
+def paths_raise(chunk, device_axis):
+    return lax.all_gather(chunk, device_axis).sum(axis=0)
+
+
+outputs_draft = functools.partial(paths_raise, device_axis=("fx", "fy"))
 
 
 def with_halo(cells, sides, width):
@@ -141,7 +149,7 @@
 
 
 def global_sums(values):
-    return lax.psum(values, ("fx", "fy"))
+    return outputs_draft(values)
 
 
 def stiffness(field_values, couplings, sparsity_layout, selector, diagonal):

time: 1010 us -> 967 us (0.957)
  blocking collectives: 535 us -> 478 us
    psum x8 -> x0, blocking collectives: 535 us -> none  [global_sums(): return lax.psum(values, ('fx', 'fy'))]
    unnamed x0 -> x6, blocking collectives: none -> 409 us
    all_gather x0 -> x2, blocking collectives: none -> 68.7 us  [paths_raise(): return lax.all_gather(chunk, device_axis).sum(axis=0)]
  transfers between devices with their start and end apart: 22 -> 22, of which waited for: 8 -> 8; matrix products, arithmetic and copies ran while one was open for 29% -> 30% of each run, Pallas kernels for 0% -> 0%
where the time goes in v1:
time: 967 us; the launch traced here: 959 us
  blocking collectives  478 us (49%)
  matrix products  127 us (13%)
  local copies, waits for them, and re-layouts  119 us (12%)
  other arithmetic  118 us (12%)
  starting transfers between devices  73.4 us (8%)
  waiting for transfers between devices  34.1 us (4%)
    unnamed x6, blocking collectives  409 us
    all_gather x2, blocking collectives, paths_raise(): return lax.all_gather(chunk, device_axis).sum(axis=0)  68.7 us
    dot_general x2, matrix products, owner_motion(): jnp.einsum('gkij,gkcj->gci', kernels, field_values[support], precision=TO...  63.6 us
    dynamic_update_slice x16, other arithmetic, owner_kernels(): lax.map(one_group, (places.reshape(-1, group, 3, points), support.reshape...  43.5 us
    dot_general x2, matrix products, owner_loads(): jnp.einsum('gkij,gci->gkcj', kernels, traction, precision=TOP_PRECISION)  39.3 us
    scatter x4, local copies, waits for them, and re-layouts, pack(): jnp.zeros((width,) + values.shape[1:], values.dtype).at[slots].set(values)  38.3 us
    all_to_all x4, waiting for transfers between devices, route_field(): lax.all_to_all(values, ('fx', 'fy'), split_axis=0, concat_axis=0, tiled=T...  30.8 us
    all_to_all x4, starting transfers between devices, route_field(): lax.all_to_all(values, ('fx', 'fy'), split_axis=0, concat_axis=0, tiled=T...  28.9 us
  transfers between devices with their start and end apart: 22, of which 8 were waited for; matrix products, arithmetic and copies ran while one was open for 30% of the time, Pallas kernels for 0%

profile of v1, /device:TPU:1, one launch (start us, length us, event | category | flops | bytes accessed | tf_op | source)
XLA Modules:
  0.0 959.1 jit_solution(6957689528994456781)
XLA Ops:
  6.5 11.5 %all-to-all-start = ((s32[128,2,2]{1,2,0:T(2,128)}), s32[128,2,2]{1,2,0:T(2,128)S(1)}, u32[]{:S(2)}, u32[]{:S(2)}) async-start(s32[128,2,2]{1,2,0:T(2,128)} %copy.346), calls=%async_computation | async-start | bytes 262144 | tf_op jit(solution)/shard_map/all_to_all | solution.py:142
  19.6 5.4 collective-permute-start.1
  32.7 12.5 %scatter_fusion = f32[256,3,128]{2,1,0:T(4,128)} fusion(f32[256,3,128]{2,1,0:T(4,128)} %broadcast.438.clone, s32[128]{0:T(128)S(1)} %fusion.166, f32[128,3,128]{2,1,0:T(4,128)S(1)} %copy.350), kind=kCustom, calls=%fused_computation.12 | custom fusion | bytes 590336 | tf_op jit(solution)/shard_map/scatter | solution.py:222
  45.2 14.9 %all-to-all-start.1 = ((f32[256,3,128]{2,1,0:T(4,128)}), f32[256,3,128]{2,1,0:T(4,128)}, u32[]{:S(2)}, u32[]{:S(2)}) async-start(f32[256,3,128]{2,1,0:T(4,128)} %scatter_fusion), calls=%async_computation.1 | async-start | bytes 1048576 | tf_op jit(solution)/shard_map/all_to_all | solution.py:141
  64.9 3.3 fusion.182
  70.3 3.3 copy.338
  75.2 3.9 copy.339
  87.0 3.2 copy.340
  93.5 5.9 pad_maximum_fusion
  112.5 69.4 %while.20 = (s32[]{:T(128)}, f32[16,16,2,128,128]{4,3,2,1,0:T(8,128)}, f32[16,16,3,128]{3,1,2,0:T(8,128)}, s32[16,16,2]{1,0,2:T(8,128)S(1)}, f32[8,3,128]{2,1,0:T(4,128)S(1)}, /*index=5*/s32[]{:T(128)}) while((s32[]{:T(128)}, f32[16,16,2,128,128]{4,3,2,1,0:T(8,128)}, f32[16,16,3,128]{3,1,2,0:T(8,128)}, s32[16,16,2]{1,0,2:T(8,128)S(1)}, ...), condition=%wide.region_5.6_spmd, body=%wide.region_4.5_spmd.sunk | while | flops 8389730 | bytes 2471257 | solution.py:121
  181.9 32.0 %convolution_bitcast_fusion.3 = f32[256,3,128]{2,1,0:T(4,128)} fusion(f32[256,2,128,128]{3,2,1,0:T(8,128)} %bitcast.475, f32[256,2,3,128]{3,1,0,2:T(2,128)S(1)} %bitcast.481), kind=kOutput, calls=%fused_computation.76 | convolution fusion | flops 301989888 | bytes 34734080 | tf_op jit(solution)/shard_map/gkij,gkcj->gci/dot_general | solution.py:128
  213.9 10.2 %all-to-all-start.2 = ((f32[256,3,128]{2,1,0:T(4,128)}), f32[256,3,128]{2,1,0:T(4,128)}, u32[]{:S(2)}, u32[]{:S(2)}) async-start(f32[256,3,128]{2,1,0:T(4,128)} %convolution_bitcast_fusion.3), calls=%async_computation.2 | async-start | bytes 1048576 | tf_op jit(solution)/shard_map/all_to_all | solution.py:148
  224.2 11.7 %fusion.4 = f32[5,8,128,129]{3,2,1,0:T(8,128)} fusion(f32[5,8,130,1]{3,2,1,0:T(8,128)} %copy.340, f32[5,8,1,128]{3,2,1,0:T(1,128)S(1)} %bitcast.492, f32[5,8,128,128]{3,2,1,0:T(8,128)} %param.40, f32[5,8,1,128]{3,2,1,0:T(1,128)S(1)} %bitcast.497, f32[5,8,130,1]{3,2,1,0:T(8,128)} %copy.341, f32[5,8,128,130]{3,2,1,0:T(8,128)} %fusion.25, f32[8,128,129]{2,1,0:T(8,128)} %fusion.24), kind=kLoop, calls=%fused_computation.29 | loop fusion | flops 7265280 | bytes 11158144 | tf_op jit(solution)/shard_map/sub | solution.py:61
  252.0 12.5 %scatter_fusion.1 = f32[256,3,128]{2,1,0:T(4,128)} fusion(f32[256,3,128]{2,1,0:T(4,128)} %broadcast.438.clone.1, s32[128]{0:T(128)S(1)} %fusion.166, f32[128,3,128]{2,1,0:T(4,128)S(1)} %copy.358), kind=kCustom, calls=%fused_computation.13 | custom fusion | bytes 590336 | tf_op jit(solution)/shard_map/scatter | solution.py:222
  264.5 9.2 all-to-all-start.3
  276.6 10.5 %all-to-all-done.3 = f32[256,3,128]{2,1,0:T(4,128)S(1)} async-done(((f32[256,3,128]{2,1,0:T(4,128)}), f32[256,3,128]{2,1,0:T(4,128)S(1)}, u32[]{:S(2)}, u32[]{:S(2)}) %all-to-all-start.3) | async-done | bytes 393248 | tf_op jit(solution)/shard_map/all_to_all | solution.py:148
  287.1 19.6 %convolution_bitcast_fusion.1 = f32[256,2,3,128]{3,2,1,0:T(4,128)S(1)} fusion(f32[256,2,128,128]{3,2,1,0:T(8,128)} %bitcast.476, f32[256,3,128]{2,1,0:T(4,128)S(1)} %all-to-all-done.3), kind=kOutput, calls=%fused_computation.74 | convolution fusion | flops 301989888 | bytes 34734080 | tf_op jit(solution)/shard_map/gkij,gci->gkcj/dot_general | solution.py:132
  315.6 71.6 %all-reduce.9 = (f32[128]{0:T(128)S(1)}, f32[128]{0:T(128)S(1)}) all-reduce(f32[128]{0:T(128)S(1)} %dynamic-update-slice.34, f32[128]{0:T(128)S(1)} %dynamic-update-slice.35), channel_id=1, replica_groups=mesh['fx'=16,'fy'=8] {'fx','fy'}, use_global_device_ids=true, to_apply=%add | all-reduce | flops 256 | bytes 2048
  391.1 62.7 %all-reduce.2 = f32[128]{0:T(128)S(1)} all-reduce(f32[128]{0:T(128)S(1)} %dynamic-update-slice.36), channel_id=1, replica_groups=mesh['fx'=16,'fy'=8] {'fx','fy'}, use_global_device_ids=true, to_apply=%add.2 | all-reduce | flops 128 | bytes 1024
  463.5 70.3 %all-reduce.3 = f32[128]{0:T(128)S(1)} all-reduce(f32[128]{0:T(128)S(1)} %dynamic-update-slice.37), channel_id=1, replica_groups=mesh['fx'=16,'fy'=8] {'fx','fy'}, use_global_device_ids=true, to_apply=%add.3 | all-reduce | flops 128 | bytes 1024
  536.1 34.4 %all-gather = f32[1024,9]{1,0:T(8,128)S(1)} all-gather(f32[8,9]{1,0:T(8,128)S(1)} %pad_maximum_fusion.17), channel_id=2, replica_groups=mesh['fx'=16,'fy'=8] {'fx','fy'}, dimensions={0}, use_global_device_ids=true | all-gather | bytes 37152 | tf_op jit(solution)/shard_map/all_gather | solution.py:20
  576.4 31.6 %convolution_bitcast_fusion.2 = f32[256,3,128]{2,1,0:T(4,128)} fusion(f32[256,2,3,128]{3,2,1,0:T(4,128)S(1)} %bitcast.482, f32[256,2,128,128]{3,2,1,0:T(8,128)} %bitcast.477), kind=kOutput, calls=%fused_computation.75 | convolution fusion | flops 301989888 | bytes 34734080 | tf_op jit(solution)/shard_map/gkij,gkcj->gci/dot_general | solution.py:128
  608.0 5.0 all-to-all-start.4
  615.9 10.9 %all-to-all-done.4 = f32[256,3,128]{2,1,0:T(4,128)S(1)} async-done(((f32[256,3,128]{2,1,0:T(4,128)}), f32[256,3,128]{2,1,0:T(4,128)S(1)}, u32[]{:S(2)}, u32[]{:S(2)}) %all-to-all-start.4) | async-done | bytes 393248 | tf_op jit(solution)/shard_map/all_to_all | solution.py:148
  641.2 12.5 %scatter_fusion.2 = f32[256,3,128]{2,1,0:T(4,128)} fusion(f32[256,3,128]{2,1,0:T(4,128)} %broadcast.438, s32[128]{0:T(128)S(1)} %copy-done.27, f32[128,3,128]{2,1,0:T(4,128)S(1)} %copy.382), kind=kCustom, calls=%fused_computation.14 | custom fusion | bytes 590336 | tf_op jit(solution)/shard_map/scatter | solution.py:222
  653.6 4.5 all-to-all-start.5
  663.4 8.2 all-to-all-done.5
  671.6 19.6 %convolution_bitcast_fusion = f32[256,2,3,128]{3,2,1,0:T(4,128)S(1)} fusion(f32[256,2,128,128]{3,2,1,0:T(8,128)} %bitcast.478, f32[256,3,128]{2,1,0:T(4,128)S(1)} %all-to-all-done.5), kind=kOutput, calls=%fused_computation.73 | convolution fusion | flops 301989888 | bytes 34734080 | tf_op jit(solution)/shard_map/gkij,gci->gkcj/dot_general | solution.py:132
  699.5 71.6 %all-reduce.8 = (f32[128]{0:T(128)S(1)}, f32[128]{0:T(128)S(1)}) all-reduce(f32[128]{0:T(128)S(1)} %dynamic-update-slice.38, f32[128]{0:T(128)S(1)} %dynamic-update-slice.39), channel_id=1, replica_groups=mesh['fx'=16,'fy'=8] {'fx','fy'}, use_global_device_ids=true, to_apply=%add.4 | all-reduce | flops 256 | bytes 2048
  775.0 62.7 %all-reduce.6 = f32[128]{0:T(128)S(1)} all-reduce(f32[128]{0:T(128)S(1)} %dynamic-update-slice.40), channel_id=1, replica_groups=mesh['fx'=16,'fy'=8] {'fx','fy'}, use_global_device_ids=true, to_apply=%add.6 | all-reduce | flops 128 | bytes 1024
  847.4 70.3 %all-reduce.7 = f32[128]{0:T(128)S(1)} all-reduce(f32[128]{0:T(128)S(1)} %dynamic-update-slice.41), channel_id=1, replica_groups=mesh['fx'=16,'fy'=8] {'fx','fy'}, use_global_device_ids=true, to_apply=%add.7 | all-reduce | flops 128 | bytes 1024
  920.4 34.4 %all-gather.1 = f32[1024,9]{1,0:T(8,128)S(1)} all-gather(f32[8,9]{1,0:T(8,128)S(1)} %pad_maximum_fusion.18), channel_id=3, replica_groups=mesh['fx'=16,'fy'=8] {'fx','fy'}, dimensions={0}, use_global_device_ids=true | all-gather | bytes 37152 | tf_op jit(solution)/shard_map/all_gather | solution.py:20
  (440 shorter events, 209.4 us)
Async XLA Ops:
  0.7 30.8 %copy-start.18 = (f32[128,3,128]{2,0,1:T(8,128)S(1)}, f32[128,3,128]{2,0,1:T(8,128)}, u32[]{:S(2)}) copy-start(f32[128,3,128]{2,0,1:T(8,128)} %param.41) | copy-start | bytes 589828
  3.3 248.8 %copy-start.26 = (s32[128]{0:T(128)}, s32[128]{0:T(128)S(1)}, u32[]{:S(2)}) copy-start(s32[128]{0:T(128)S(1)} %fusion.166) | copy-start | bytes 1540
  6.5 38.7 %all-to-all-start = ((s32[128,2,2]{1,2,0:T(2,128)}), s32[128,2,2]{1,2,0:T(2,128)S(1)}, u32[]{:S(2)}, u32[]{:S(2)}) async-start(s32[128,2,2]{1,2,0:T(2,128)} %copy.346), calls=%async_computation | async-start | bytes 262144 | tf_op jit(solution)/shard_map/all_to_all | solution.py:142
  19.6 43.3 %collective-permute-start.1 = (f32[5,8,1,128]{3,1,2,0:T(8,128)}, f32[5,8,1,128]{3,1,2,0:T(8,128)S(1)}, u32[]{:S(2)}, u32[]{:S(2)}) collective-permute-start(f32[5,8,1,128]{3,1,2,0:T(8,128)} %bitcast.174), channel_id=1, source_target_pairs={{8,0},{16,8},{24,16},{32,24},{40,32},{48,40},{56,48},{64,56},{72,6... | collective-permute-start | bytes 61448 | tf_op jit(solution)/shard_map/ppermute | solution.py:35
  25.0 37.9 %collective-permute-start = (f32[5,8,1,128]{3,1,2,0:T(8,128)}, f32[5,8,1,128]{3,1,2,0:T(8,128)S(1)}, u32[]{:S(2)}, u32[]{:S(2)}) collective-permute-start(f32[5,8,1,128]{3,1,2,0:T(8,128)} %bitcast.173), channel_id=1, source_target_pairs={{0,8},{8,16},{16,24},{24,32},{32,40},{40,48},{48,56},{56,64},{64,7... | collective-permute-start | bytes 61448 | tf_op jit(solution)/shard_map/ppermute | solution.py:33
  27.7 279.0 %collective-permute-start.5 = (f32[8,3,128]{2,0,1:T(8,128)}, f32[8,3,128]{2,0,1:T(8,128)}, u32[]{:S(2)}, u32[]{:S(2)}) collective-permute-start(f32[8,3,128]{2,0,1:T(8,128)} %convolution_bitcast_fusion.22), channel_id=1, source_target_pairs={{1,0},{2,1},{3,2},{4,3},{5,4},{6,5},{7,6},{8,7},{9,8},{10,9},{11,1... | collective-permute-start | bytes 36872 | tf_op jit(solution)/shard_map/ppermute | solution.py:35
  28.3 245.8 %collective-permute-start.4 = (f32[8,3,128]{2,1,0:T(4,128)S(1)}, f32[8,3,128]{2,1,0:T(4,128)S(1)}, u32[]{:S(2)}, u32[]{:S(2)}) collective-permute-start(f32[8,3,128]{2,1,0:T(4,128)S(1)} %copy.360), channel_id=1, source_target_pairs={{0,1},{1,2},{2,3},{3,4},{4,5},{5,6},{6,7},{7,8},{8,9},{9,10},{10,1... | collective-permute-start | bytes 36872 | tf_op jit(solution)/shard_map/ppermute | solution.py:33
  30.7 29.9 %copy-start.9 = (f32[5,1,128,128]{3,2,1,0:T(8,128)}, f32[5,1,128,128]{3,2,1,0:T(8,128)S(1)}, u32[]{:S(2)}) copy-start(f32[5,1,128,128]{3,2,1,0:T(8,128)S(1)} %get-tuple-element.234) | copy-start | bytes 983044
  30.7 206.4 %copy-start.28 = (s32[1024]{0:T(1024)}, s32[1024]{0:T(1024)S(1)}, u32[]{:S(2)}) copy-start(s32[1024]{0:T(1024)S(1)} %pad_clamp_fusion.2) | copy-start | bytes 12292
  45.2 65.5 %all-to-all-start.1 = ((f32[256,3,128]{2,1,0:T(4,128)}), f32[256,3,128]{2,1,0:T(4,128)}, u32[]{:S(2)}, u32[]{:S(2)}) async-start(f32[256,3,128]{2,1,0:T(4,128)} %scatter_fusion), calls=%async_computation.1 | async-start | bytes 1048576 | tf_op jit(solution)/shard_map/all_to_all | solution.py:141
  73.6 13.5 %collective-permute-start.2 = (f32[5,8,130,1]{2,1,3,0:T(8,128)S(1)}, f32[5,8,130,1]{2,1,3,0:T(8,128)}, u32[]{:S(2)}, u32[]{:S(2)}) collective-permute-start(f32[5,8,130,1]{2,1,3,0:T(8,128)S(1)} %copy.338), channel_id=1, source_target_pairs={{0,1},{1,2},{2,3},{3,4},{4,5},{5,6},{6,7},{7,0},{8,9},{9,10},{10,1... | collective-permute-start | bytes 62408 | tf_op jit(solution)/shard_map/ppermute | solution.py:33
  79.1 11.2 %collective-permute-start.3 = (f32[5,8,130,1]{2,1,3,0:T(8,128)}, f32[5,8,130,1]{2,1,3,0:T(8,128)}, u32[]{:S(2)}, u32[]{:S(2)}) collective-permute-start(f32[5,8,130,1]{2,1,3,0:T(8,128)} %copy.339), channel_id=1, source_target_pairs={{1,0},{2,1},{3,2},{4,3},{5,4},{6,5},{7,6},{0,7},{9,8},{10,9},{11,1... | collective-permute-start | bytes 62408 | tf_op jit(solution)/shard_map/ppermute | solution.py:35
  213.9 23.2 %all-to-all-start.2 = ((f32[256,3,128]{2,1,0:T(4,128)}), f32[256,3,128]{2,1,0:T(4,128)}, u32[]{:S(2)}, u32[]{:S(2)}) async-start(f32[256,3,128]{2,1,0:T(4,128)} %convolution_bitcast_fusion.3), calls=%async_computation.2 | async-start | bytes 1048576 | tf_op jit(solution)/shard_map/all_to_all | solution.py:148
  264.5 22.6 %all-to-all-start.3 = ((f32[256,3,128]{2,1,0:T(4,128)}), f32[256,3,128]{2,1,0:T(4,128)S(1)}, u32[]{:S(2)}, u32[]{:S(2)}) async-start(f32[256,3,128]{2,1,0:T(4,128)} %scatter_fusion.1), calls=%async_computation.3 | async-start | bytes 1048576 | tf_op jit(solution)/shard_map/all_to_all | solution.py:148
  274.1 32.6 %copy-start.23 = (s32[256,2]{0,1:T(2,128)}, s32[256,2]{0,1:T(2,128)S(1)}, u32[]{:S(2)}) copy-start(s32[256,2]{0,1:T(2,128)S(1)} %eq.26) | copy-start | bytes 6148
  276.6 30.1 %copy-start.19 = (f32[8,128]{1,0:T(8,128)S(1)}, f32[8,128]{1,0:T(8,128)}, u32[]{:S(2)}) copy-start(f32[8,128]{1,0:T(8,128)} %param.48) | copy-start | bytes 12292
  276.6 30.1 %copy-start.22 = (f32[8,3,128]{2,0,1:T(8,128)S(1)}, f32[8,3,128]{2,0,1:T(8,128)}, u32[]{:S(2)}) copy-start(f32[8,3,128]{2,0,1:T(8,128)} %param.49) | copy-start | bytes 36868
  307.9 2.5 collective-permute-start.6
  310.3 3.1 collective-permute-start.7
  455.7 3.0 collective-permute-start.8
  457.4 116.4 %copy-start.17 = (f32[8,8,3,128]{3,1,2,0:T(8,128)S(1)}, f32[8,8,3,128]{3,1,2,0:T(8,128)}, u32[]{:S(2)}) copy-start(f32[8,8,3,128]{3,1,2,0:T(8,128)} %param.52) | copy-start | bytes 294916
  458.7 3.4 collective-permute-start.9
  608.0 18.8 %all-to-all-start.4 = ((f32[256,3,128]{2,1,0:T(4,128)}), f32[256,3,128]{2,1,0:T(4,128)S(1)}, u32[]{:S(2)}, u32[]{:S(2)}) async-start(f32[256,3,128]{2,1,0:T(4,128)} %convolution_bitcast_fusion.2), calls=%async_computation.4 | async-start | bytes 1048576 | tf_op jit(solution)/shard_map/all_to_all | solution.py:148
  614.0 47.0 %collective-permute-start.10 = (f32[8,3,128]{2,0,1:T(8,128)S(1)}, f32[8,3,128]{2,0,1:T(8,128)S(1)}, u32[]{:S(2)}, u32[]{:S(2)}) collective-permute-start(f32[8,3,128]{2,0,1:T(8,128)S(1)} %bitcast_subtract_fusion.1), channel_id=1, source_target_pairs={{0,1},{1,2},{2,3},{3,4},{4,5},{5,6},{6,7},{7,8},{8,9},{9,10},{10,1... | collective-permute-start | bytes 36872 | tf_op jit(solution)/shard_map/ppermute | solution.py:33
  653.6 18.0 %all-to-all-start.5 = ((f32[256,3,128]{2,1,0:T(4,128)}), f32[256,3,128]{2,1,0:T(4,128)S(1)}, u32[]{:S(2)}, u32[]{:S(2)}) async-start(f32[256,3,128]{2,1,0:T(4,128)} %scatter_fusion.2), calls=%async_computation.5 | async-start | bytes 1048576 | tf_op jit(solution)/shard_map/all_to_all | solution.py:148
  659.4 31.9 %collective-permute-start.11 = (f32[8,3,128]{2,0,1:T(8,128)S(1)}, f32[8,3,128]{2,0,1:T(8,128)S(1)}, u32[]{:S(2)}, u32[]{:S(2)}) collective-permute-start(f32[8,3,128]{2,0,1:T(8,128)S(1)} %convolution_bitcast_fusion.18), channel_id=1, source_target_pairs={{1,0},{2,1},{3,2},{4,3},{5,4},{6,5},{7,6},{8,7},{9,8},{10,9},{11,1... | collective-permute-start | bytes 36872 | tf_op jit(solution)/shard_map/ppermute | solution.py:35
  691.7 2.5 collective-permute-start.12
  694.2 3.1 collective-permute-start.13
  839.6 3.0 collective-permute-start.14
  841.3 116.8 %slice-start.2 = ((f32[8,8,3,128]{3,1,2,0:T(8,128)}), f32[7,8,3,128]{3,1,2,0:T(8,128)S(1)}, s32[]{:S(2)}) async-start(f32[8,8,3,128]{3,1,2,0:T(8,128)} %param.52), calls=%async_computation.8 | async-start | bytes 172032 | tf_op jit(solution)/shard_map/slice | solution.py:257
  842.6 3.4 collective-permute-start.15
  919.7 39.3 %copy-start.21 = (f32[8,3,128]{2,0,1:T(8,128)}, f32[8,3,128]{2,0,1:T(8,128)S(1)}, u32[]{:S(2)}) copy-start(f32[8,3,128]{2,0,1:T(8,128)S(1)} %get-tuple-element.209) | copy-start | bytes 36868
  (22 other events, 221.1 us)
